TPU v7x, 32 devices: a whole 2x2x4 slice. The times are simulated.
32 devices in a mesh: param: 8 (over y, x, core), ex: 4 (over z).
Axes of the slice: x: 2, y: 2, z: 4, core: 2. Of those that a mesh axis runs over, the one named last changes fastest.
Arguments:
- grads: float32 [49152, 2048], P('param', 'ex'), may hold values from -6 to 6
- projection: bfloat16 [49152, 1024], P('param'), may hold values from -6 to 6
- whitener: float32 [1024, 1024], P('param'), may hold values from -1 to 3
Outputs:
- scores: float32 [2048, 2048], P('ex', 'param')
All inputs are finite; a program needn't handle non-finite values.
Results may differ from a plain program's by a relative error of at most 0.0052.
Values may be sent and summed in bfloat16 or wider, within the bound.
A program may use at most 128 MiB of HBM per device.

v0:
```python
import math
import jax
import jax.numpy as jnp
from jax import lax
from jax.sharding import PartitionSpec as P


def body(grads, projection, whitener):
    low_grads = grads.astype(jnp.bfloat16)
    partial_value = lax.dot_general(
        projection, low_grads, (((0,), (0,)), ((), ())), preferred_element_type=jnp.float32
    )
    param_count = lax.axis_size("param")
    ex_count = lax.axis_size("ex")
    norm_factor = 1.0 / math.sqrt(grads.shape[0] * param_count)
    whole_whitener = lax.all_gather(whitener, "param", axis=0, tiled=True)
    sketch_rows = partial_value.shape[0]
    local_width = grads.shape[1]
    total_width = local_width * ex_count
    tile_width = total_width // param_count
    col_start = lax.axis_index("param") * tile_width
    owned_share = (
        lax.psum_scatter(partial_value, "param", scatter_dimension=1, tiled=True) * norm_factor
    )
    whitened = jnp.dot(whole_whitener, owned_share, precision=lax.Precision.HIGHEST).astype(
        jnp.bfloat16
    )
    joined = lax.all_gather(whitened, ("param", "ex"), axis=1, tiled=True)
    piece_width = owned_share.shape[1]
    all_columns = joined.reshape(sketch_rows, param_count, ex_count, piece_width)
    all_columns = all_columns.transpose(0, 2, 1, 3).reshape(
        sketch_rows, param_count * ex_count * piece_width
    )
    row_start = lax.axis_index("ex") * local_width
    row_block = lax.dynamic_slice_in_dim(all_columns, row_start, local_width, 1)
    col_block = lax.dynamic_slice_in_dim(all_columns, col_start, tile_width, 1)
    tile = lax.dot_general(
        row_block, col_block, (((0,), (0,)), ((), ())), preferred_element_type=jnp.float32
    )
    return tile / sketch_rows


def solution(mesh):
    return jax.shard_map(
        body,
        mesh=mesh,
        in_specs=(P("param", "ex"), P("param", None), P("param", None)),
        out_specs=P("ex", "param"),
        check_vma=False,
    )
```

profile of v0, /device:TPU:0, one launch (start us, length us, event | category | flops | bytes accessed | tf_op | source)
XLA Modules:
  0.0 182.8 jit_solution(3519660130798700273)
XLA Ops:
  6.5 0.0 reduce-scatter.4.cloned.1.call-start
  6.5 14.3 %fusion.2 = f32[512,1024]{1,0:T(8,128)} fusion(bf16[6144,1024]{1,0:T(8,128)(2,1)} %param.4, f32[6144,512]{1,0:T(8,128)} %param.3), kind=kOutput, calls=%fused_computation.2 | convolution fusion | flops 6445596672 | bytes 27262976
  20.9 0.0 reduce-scatter.4.cloned.1.call-update
  20.9 0.0 all-gather.3.cloned.1.call-start
  20.9 0.7 all-gather.3.cloned.1.call-update
  21.6 0.0 all-gather.5.cloned.1.call-start
  21.7 43.2 %reduce-scatter.4.cloned.1.call-done = f32[64,1024]{1,0:T(8,128)} async-done(((f32[512,1024]{1,0:T(8,128)}), f32[64,1024]{1,0:T(8,128)}) %reduce-scatter.4.cloned.1.call-update) | async-done | bytes 262160
  64.9 1.1 copy.9
  66.0 37.3 %all-gather.3.cloned.1.call-done = f32[1024,1024]{1,0:T(8,128)} async-done(((f32[128,1024]{1,0:T(8,128)}), f32[1024,1024]{1,0:T(8,128)}) %all-gather.3.cloned.1.call-update) | async-done | bytes 4194320 | tf_op jit(solution)/shard_map/all_gather | solution.py:16
  103.4 7.2 %fusion.5 = bf16[1024,64]{0,1:T(8,128)(2,1)} fusion(f32[1024,1024]{1,0:T(8,128)} %all-gather.3.cloned.1.call-done, f32[1024,64]{1,0:T(8,128)S(1)} %copy.9), kind=kOutput, calls=%fused_computation.5 | convolution fusion | flops 805437440 | bytes 4587520 | tf_op jit(solution)/shard_map/dot_general | solution.py:25
  110.5 0.0 all-gather.5.cloned.1.call-update
  110.6 61.8 %all-gather.5.cloned.1.call-done = bf16[1024,2048]{0,1:T(8,128)(2,1)} async-done(((bf16[1024,64]{0,1:T(8,128)(2,1)}), bf16[1024,2048]{0,1:T(8,128)(2,1)}) %all-gather.5.cloned.1.call-update) | async-done | bytes 4194320 | tf_op jit(solution)/shard_map/all_gather | solution.py:28
  172.3 2.6 %copy.6 = bf16[1024,8,4,64]{0,3,1,2:T(8,128)(2,1)S(1)} copy(bf16[1024,8,4,64]{0,3,2,1:T(8,128)(2,1)} %bitcast.12) | data formatting | bytes 8388608 | tf_op jit(solution)/shard_map/reshape | solution.py:30
  175.0 1.3 convolution_multiply_fusion
Async XLA Ops:
  6.5 58.3 %reduce-scatter.4.cloned.1.call-start = ((), (), s32[]{:S(2)}) async-start(), calls=%async_computation.3 | async-start | bytes 2359296
  20.9 82.5 %all-gather.3.cloned.1.call-start = ((), (), s32[]{:S(2)}) async-start(), calls=%async_computation.1 | async-start | bytes 4718592 | tf_op jit(solution)/shard_map/all_gather | solution.py:16
  21.6 150.7 %all-gather.5.cloned.1.call-start = ((), (), s32[]{:S(2)}) async-start(), calls=%async_computation.2 | async-start | bytes 4325376 | tf_op jit(solution)/shard_map/all_gather | solution.py:28
Sparse Core Ops, SparseCore 0:
  21.0 43.8 reduce-scatter.3
  66.8 36.5 all-gather.2
  110.7 61.6 all-gather.4
where the time goes:
time: 183 us
  waiting for transfers between devices  143 us (78%)
  matrix products  22.8 us (12%)
  between operations  13.1 us (7%)
  local copies, waits for them, and re-layouts  3.77 us (2%)
    all_gather x1, waiting for transfers between devices, body(): joined = lax.all_gather(whitened, ('param', 'ex'), axis=1, tiled=True)  61.8 us
    unnamed x4, waiting for transfers between devices  43.9 us
    all_gather x1, waiting for transfers between devices, body(): whole_whitener = lax.all_gather(whitener, 'param', axis=0, tiled=True)  37.3 us
    unnamed x1, matrix products  14.3 us
    dot_general x1, matrix products, body(): jnp.dot(whole_whitener, owned_share, precision=lax.Precision.HIGHEST)  7.16 us
  transfers between devices with their start and end apart: 3, of which 3 were waited for; matrix products, arithmetic and copies ran while one was open for 1% of the time, Pallas kernels for 0%

commit v1 on v0

--- a/solution.py
+++ b/solution.py
@@ -13,7 +13,15 @@
     param_count = lax.axis_size("param")
     ex_count = lax.axis_size("ex")
     norm_factor = 1.0 / math.sqrt(grads.shape[0] * param_count)
-    whole_whitener = lax.all_gather(whitener, "param", axis=0, tiled=True)
+    count = lax.axis_size("param")
+    held, blocks = (whitener, [whitener])
+    for _ in range(count - 1):
+        held = lax.ppermute(held, "param", [(i, (i + 1) % count) for i in range(count)])
+        blocks.insert(0, held)
+    row_of_blocks = jnp.concatenate(blocks, axis=0)
+    whole_whitener = jnp.roll(
+        row_of_blocks, (lax.axis_index("param") + 1) * whitener.shape[0], axis=0
+    )
     sketch_rows = partial_value.shape[0]
     local_width = grads.shape[1]
     total_width = local_width * ex_count

time: 183 us -> 173 us (0.945)
  waiting for transfers between devices: 143 us -> 127 us
  local copies, waits for them, and re-layouts: 3.77 us -> 10.4 us
  matrix products: 22.8 us -> 20.5 us
  starting transfers between devices: 0.08 us -> 2.06 us
    ppermute x0 -> x7, waiting for transfers between devices: none -> 55.3 us  [body(): lax.ppermute(held, 'param', [(i, (i + 1) % count) for i in range(count)])]
    unnamed x4 -> x3, waiting for transfers between devices: 43.9 us -> 4.48 us
    all_gather x1 -> x0, waiting for transfers between devices: 37.3 us -> none  [body(): whole_whitener = lax.all_gather(whitener, 'param', axis=0, tiled=True)]
    unnamed x1 -> x22, local copies, waits for them, and re-layouts: 1.14 us -> 7.71 us
    all_gather x1, waiting for transfers between devices: 61.8 us -> 66.8 us  [body(): joined = lax.all_gather(whitened, ('param', 'ex'), axis=1, tiled=True)]
    dot_general x1, matrix products: 7.16 us -> 4.91 us  [body(): jnp.dot(whole_whitener, owned_share, precision=lax.Precision.HIGHEST)]
    ppermute x0 -> x7, starting transfers between devices: none -> 2.02 us  [body(): lax.ppermute(held, 'param', [(i, (i + 1) % count) for i in range(count)])]
  transfers between devices with their start and end apart: 3 -> 9, of which waited for: 3 -> 8; matrix products, arithmetic and copies ran while one was open for 1% -> 9% of each run, Pallas kernels for 0% -> 0%
where the time goes in v1:
time: 173 us
  waiting for transfers between devices  127 us (73%)
  matrix products  20.5 us (12%)
  between operations  13.6 us (8%)
  local copies, waits for them, and re-layouts  10.4 us (6%)
  starting transfers between devices  2.06 us (1%)
    all_gather x1, waiting for transfers between devices, body(): joined = lax.all_gather(whitened, ('param', 'ex'), axis=1, tiled=True)  66.8 us
    ppermute x7, waiting for transfers between devices, body(): lax.ppermute(held, 'param', [(i, (i + 1) % count) for i in range(count)])  55.3 us
    unnamed x1, matrix products  14.3 us
    unnamed x22, local copies, waits for them, and re-layouts  7.71 us
    dot_general x1, matrix products, body(): jnp.dot(whole_whitener, owned_share, precision=lax.Precision.HIGHEST)  4.91 us
    unnamed x3, waiting for transfers between devices  4.48 us
  transfers between devices with their start and end apart: 9, of which 8 were waited for; matrix products, arithmetic and copies ran while one was open for 9% of the time, Pallas kernels for 0%

profile of v1, /device:TPU:0, one launch (start us, length us, event | category | flops | bytes accessed | tf_op | source)
XLA Modules:
  0.0 173.1 jit_solution(5415028639301929488)
XLA Ops:
  6.5 0.0 reduce-scatter.4.cloned.1.call-start
  6.5 0.5 collective-permute-start
  7.0 9.9 %collective-permute-done = f32[128,1024]{1,0:T(8,128)S(1)} collective-permute-done((f32[128,1024]{1,0:T(8,128)}, f32[128,1024]{1,0:T(8,128)S(1)}, u32[]{:S(2)}, u32[]{:S(2)}) %collective-permute-start) | collective-permute-done | bytes 524320 | tf_op jit(solution)/shard_map/ppermute | solution.py:19
  17.0 0.0 collective-permute-start.1
  17.0 14.3 %fusion.4 = f32[512,1024]{1,0:T(8,128)} fusion(bf16[6144,1024]{1,0:T(8,128)(2,1)} %param.4, f32[6144,512]{1,0:T(8,128)} %param.3), kind=kOutput, calls=%fused_computation.4 | convolution fusion | flops 6445596672 | bytes 27262976
  31.3 0.0 copy-start
  31.3 0.0 reduce-scatter.4.cloned.1.call-update
  31.3 0.0 all-gather.2.cloned.1.call-start
  31.4 0.0 collective-permute-done.1
  31.4 1.5 collective-permute-start.2
  32.9 8.0 %collective-permute-done.2 = f32[128,1024]{1,0:T(8,128)S(1)} collective-permute-done((f32[128,1024]{1,0:T(8,128)S(1)}, f32[128,1024]{1,0:T(8,128)S(1)}, u32[]{:S(2)}, u32[]{:S(2)}) %collective-permute-start.2) | collective-permute-done | bytes 524320 | tf_op jit(solution)/shard_map/ppermute | solution.py:19
  40.9 0.0 collective-permute-start.3
  40.9 9.5 %collective-permute-done.3 = f32[128,1024]{1,0:T(8,128)S(1)} collective-permute-done((f32[128,1024]{1,0:T(8,128)S(1)}, f32[128,1024]{1,0:T(8,128)S(1)}, u32[]{:S(2)}, u32[]{:S(2)}) %collective-permute-start.3) | collective-permute-done | bytes 524320 | tf_op jit(solution)/shard_map/ppermute | solution.py:19
  50.4 0.0 collective-permute-start.4
  50.5 13.9 %collective-permute-done.4 = f32[128,1024]{1,0:T(8,128)S(1)} collective-permute-done((f32[128,1024]{1,0:T(8,128)S(1)}, f32[128,1024]{1,0:T(8,128)S(1)}, u32[]{:S(2)}, u32[]{:S(2)}) %collective-permute-start.4) | collective-permute-done | bytes 524320 | tf_op jit(solution)/shard_map/ppermute | solution.py:19
  64.4 0.0 copy-start.1
  64.4 0.8 copy-done.1
  65.2 0.0 collective-permute-start.5
  65.2 9.7 %collective-permute-done.5 = f32[128,1024]{1,0:T(8,128)} collective-permute-done((f32[128,1024]{1,0:T(8,128)S(1)}, f32[128,1024]{1,0:T(8,128)}, u32[]{:S(2)}, u32[]{:S(2)}) %collective-permute-start.5) | collective-permute-done | bytes 524320 | tf_op jit(solution)/shard_map/ppermute | solution.py:19
  74.9 0.0 collective-permute-start.6
  74.9 4.4 %reduce-scatter.4.cloned.1.call-done = f32[64,1024]{1,0:T(8,128)} async-done(((f32[512,1024]{1,0:T(8,128)}), f32[64,1024]{1,0:T(8,128)}) %reduce-scatter.4.cloned.1.call-update) | async-done | bytes 262160
  79.3 1.1 copy.9
  80.5 0.0 copy-start.2
  80.5 4.2 %collective-permute-done.6 = f32[128,1024]{1,0:T(8,128)} collective-permute-done((f32[128,1024]{1,0:T(8,128)}, f32[128,1024]{1,0:T(8,128)}, u32[]{:S(2)}, u32[]{:S(2)}) %collective-permute-start.6) | collective-permute-done | bytes 524320 | tf_op jit(solution)/shard_map/ppermute | solution.py:19
  84.7 1.1 constant_dynamic-update-slice_fusion.15
  85.8 1.1 constant_dynamic-update-slice_fusion.14
  86.9 1.1 constant_dynamic-update-slice_fusion.13
  88.1 0.0 copy-done
  88.2 1.1 constant_dynamic-update-slice_fusion.7
  89.3 1.1 constant_dynamic-update-slice_fusion.6
  90.3 0.0 copy-done.2
  90.6 4.9 %fusion.7 = bf16[1024,64]{0,1:T(8,128)(2,1)} fusion(f32[2048,1024]{1,0:T(8,128)S(1)} %constant_dynamic-update-slice_fusion, s32[]{:T(128)S(6)} %select_n.20, f32[1024,64]{1,0:T(8,128)S(1)} %copy.9), kind=kOutput, calls=%fused_computation.6 | convolution fusion | flops 805437440 | bytes 4849668 | tf_op jit(solution)/shard_map/dot_general | solution.py:33
  95.5 0.0 all-gather.2.cloned.1.call-update
  95.6 66.8 %all-gather.2.cloned.1.call-done = bf16[1024,2048]{0,1:T(8,128)(2,1)} async-done(((bf16[1024,64]{0,1:T(8,128)(2,1)}), bf16[1024,2048]{0,1:T(8,128)(2,1)}) %all-gather.2.cloned.1.call-update) | async-done | bytes 4194320 | tf_op jit(solution)/shard_map/all_gather | solution.py:36
  162.3 2.6 %copy.6 = bf16[1024,8,4,64]{0,3,1,2:T(8,128)(2,1)S(1)} copy(bf16[1024,8,4,64]{0,3,2,1:T(8,128)(2,1)} %bitcast.9) | data formatting | bytes 8388608 | tf_op jit(solution)/shard_map/reshape | solution.py:38
  165.0 1.3 convolution_multiply_fusion
  (11 shorter events, 0.4 us)
Async XLA Ops:
  6.5 72.8 %reduce-scatter.4.cloned.1.call-start = ((), (), s32[]{:S(2)}) async-start(), calls=%async_computation.2 | async-start | bytes 2359296
  6.5 10.4 %collective-permute-start = (f32[128,1024]{1,0:T(8,128)}, f32[128,1024]{1,0:T(8,128)S(1)}, u32[]{:S(2)}, u32[]{:S(2)}) collective-permute-start(f32[128,1024]{1,0:T(8,128)} %param.5), channel_id=1, source_target_pairs={{0,4},{4,8},{8,12},{12,16},{16,20},{20,24},{24,28},{28,0},{1,5},{5... | collective-permute-start | bytes 1572872 | tf_op jit(solution)/shard_map/ppermute | solution.py:19
  17.0 14.4 %collective-permute-start.1 = (f32[128,1024]{1,0:T(8,128)S(1)}, f32[128,1024]{1,0:T(8,128)S(1)}, u32[]{:S(2)}, u32[]{:S(2)}) collective-permute-start(f32[128,1024]{1,0:T(8,128)S(1)} %collective-permute-done), channel_id=1, source_target_pairs={{0,4},{4,8},{8,12},{12,16},{16,20},{20,24},{24,28},{28,0},{1,5},{5... | collective-permute-start | bytes 1572872 | tf_op jit(solution)/shard_map/ppermute | solution.py:19
  31.3 56.8 %copy-start = (f32[128,1024]{1,0:T(8,128)S(1)}, f32[128,1024]{1,0:T(8,128)}, u32[]{:S(2)}) copy-start(f32[128,1024]{1,0:T(8,128)} %param.5) | copy-start | bytes 1572868
  31.3 131.0 %all-gather.2.cloned.1.call-start = ((), (), s32[]{:S(2)}) async-start(), calls=%async_computation.1 | async-start | bytes 4325376 | tf_op jit(solution)/shard_map/all_gather | solution.py:36
  31.4 9.6 %collective-permute-start.2 = (f32[128,1024]{1,0:T(8,128)S(1)}, f32[128,1024]{1,0:T(8,128)S(1)}, u32[]{:S(2)}, u32[]{:S(2)}) collective-permute-start(f32[128,1024]{1,0:T(8,128)S(1)} %collective-permute-done.1), channel_id=1, source_target_pairs={{0,4},{4,8},{8,12},{12,16},{16,20},{20,24},{24,28},{28,0},{1,5},{5... | collective-permute-start | bytes 1572872 | tf_op jit(solution)/shard_map/ppermute | solution.py:19
  40.9 9.5 %collective-permute-start.3 = (f32[128,1024]{1,0:T(8,128)S(1)}, f32[128,1024]{1,0:T(8,128)S(1)}, u32[]{:S(2)}, u32[]{:S(2)}) collective-permute-start(f32[128,1024]{1,0:T(8,128)S(1)} %collective-permute-done.2), channel_id=1, source_target_pairs={{0,4},{4,8},{8,12},{12,16},{16,20},{20,24},{24,28},{28,0},{1,5},{5... | collective-permute-start | bytes 1572872 | tf_op jit(solution)/shard_map/ppermute | solution.py:19
  50.4 13.9 %collective-permute-start.4 = (f32[128,1024]{1,0:T(8,128)S(1)}, f32[128,1024]{1,0:T(8,128)S(1)}, u32[]{:S(2)}, u32[]{:S(2)}) collective-permute-start(f32[128,1024]{1,0:T(8,128)S(1)} %collective-permute-done.3), channel_id=1, source_target_pairs={{0,4},{4,8},{8,12},{12,16},{16,20},{20,24},{24,28},{28,0},{1,5},{5... | collective-permute-start | bytes 1572872 | tf_op jit(solution)/shard_map/ppermute | solution.py:19
  64.4 0.8 copy-start.1
  65.2 9.7 %collective-permute-start.5 = (f32[128,1024]{1,0:T(8,128)S(1)}, f32[128,1024]{1,0:T(8,128)}, u32[]{:S(2)}, u32[]{:S(2)}) collective-permute-start(f32[128,1024]{1,0:T(8,128)S(1)} %collective-permute-done.4), channel_id=1, source_target_pairs={{0,4},{4,8},{8,12},{12,16},{16,20},{20,24},{24,28},{28,0},{1,5},{5... | collective-permute-start | bytes 1572872 | tf_op jit(solution)/shard_map/ppermute | solution.py:19
  74.9 9.8 %collective-permute-start.6 = (f32[128,1024]{1,0:T(8,128)}, f32[128,1024]{1,0:T(8,128)}, u32[]{:S(2)}, u32[]{:S(2)}) collective-permute-start(f32[128,1024]{1,0:T(8,128)} %collective-permute-done.5), channel_id=1, source_target_pairs={{0,4},{4,8},{8,12},{12,16},{16,20},{20,24},{24,28},{28,0},{1,5},{5... | collective-permute-start | bytes 1572872 | tf_op jit(solution)/shard_map/ppermute | solution.py:19
  80.5 9.9 %copy-start.2 = (f32[128,1024]{1,0:T(8,128)S(1)}, f32[128,1024]{1,0:T(8,128)}, u32[]{:S(2)}) copy-start(f32[128,1024]{1,0:T(8,128)} %copy-done.1) | copy-start | bytes 1572868
Sparse Core Ops, SparseCore 0:
  31.4 47.8 reduce-scatter.3
  95.7 66.6 all-gather.1
